TPU v7x, 256 devices: a whole 4x4x8 slice. The times are simulated.
256 devices in a mesh: dp: 4 (over y), seq: 16 (over z, core), mp: 4 (over x).
Axes of the slice: x: 4, y: 4, z: 8, core: 2. Of those that a mesh axis runs over, the one named last changes fastest.
Arguments:
- q_self: bfloat16 [4, 1024, 4096], P('dp', 'seq', 'mp'), may hold values from -12 to 12
- k_self: bfloat16 [4, 1024, 4096], P('dp', 'seq', 'mp'), may hold values from -3 to 3
- v_self: bfloat16 [4, 1024, 4096], P('dp', 'seq', 'mp'), may hold values from -0.75 to 0.75
- out_grad_self: bfloat16 [4, 1024, 4096], P('dp', 'seq', 'mp'), may hold values from -6 to 6
- q_cross: bfloat16 [4, 1024, 4096], P('dp', 'seq', 'mp'), may hold values from -12 to 12
- k_cross: bfloat16 [4, 2048, 4096], P('dp', 'seq', 'mp'), may hold values from -3 to 3
- v_cross: bfloat16 [4, 2048, 4096], P('dp', 'seq', 'mp'), may hold values from -0.75 to 0.75
- out_grad_cross: bfloat16 [4, 1024, 4096], P('dp', 'seq', 'mp'), may hold values from -8 to 8
- dec_lengths: int32 [4, 16], P('dp'), may hold values from 1 to 640, as said below
- enc_lengths: int32 [4, 16], P('dp'), may hold values from 1 to 1280, as said below
- rel_bias: float32 [32, 64], P(None, 'mp'), may hold values from -4 to 4
Outputs:
- grad_q_self: bfloat16 [4, 1024, 4096], P('dp', 'seq', 'mp')
- grad_k_self: bfloat16 [4, 1024, 4096], P('dp', 'seq', 'mp')
- grad_v_self: bfloat16 [4, 1024, 4096], P('dp', 'seq', 'mp')
- grad_q_cross: bfloat16 [4, 1024, 4096], P('dp', 'seq', 'mp')
- grad_k_cross: bfloat16 [4, 2048, 4096], P('dp', 'seq', 'mp')
- grad_v_cross: bfloat16 [4, 2048, 4096], P('dp', 'seq', 'mp')
- bias_grad: float32 [32, 64], P(None, 'mp')
Inputs may be any that keep to these rules, and one draw needn't show every extreme that they name: `dec_lengths`: row p lists the decoder lengths of the 16 examples of pack p in order; they sum to 1024 and the largest is exactly 640. `enc_lengths`: row p lists the encoder lengths of the same 16 examples in the same order; they sum to 2048. The example with 640 decoder rows has exactly 1280 encoder rows; every other example has at least as many encoder rows as decoder rows and at most three times as many.
All inputs are finite; a program needn't handle non-finite values.
Results may differ from a plain program's by a relative error of at most 0.039.
Values may be sent and summed in bfloat16 or wider, within the bound.
A program may use at most 128 MiB of HBM per device.

v0:
```python
import math
import jax
import jax.numpy as jnp
from jax import lax
from jax.sharding import PartitionSpec as P

HEAD_DIM = 64
BUCKETS = 32
DISTANCE = 128


def bucket_of(distances):
    exact_count = BUCKETS // 2
    bucketed = jnp.full(distances.shape, exact_count, jnp.int32)
    for level_index in range(1, BUCKETS - exact_count):
        threshold = math.ceil(
            exact_count * (DISTANCE / exact_count) ** (level_index / (BUCKETS - exact_count))
        )
        bucketed = bucketed + (distances >= threshold).astype(jnp.int32)
    return jnp.where(distances < exact_count, distances, bucketed)


def example_ids(total_rows, lengths):
    segment_ends = jnp.cumsum(lengths)
    positions = jnp.arange(total_rows, dtype=jnp.int32)
    return jnp.sum((positions[:, None] >= segment_ends[None, :]).astype(jnp.int32), axis=1)


def distance_table(rel_bias, offset_base, table_span):
    distances = offset_base + jnp.arange(table_span, dtype=jnp.int32)
    buckets = bucket_of(jnp.maximum(distances, 0))
    one_hot = (buckets[None, :] == jnp.arange(rel_bias.shape[0], dtype=jnp.int32)[:, None]).astype(
        jnp.float32
    )
    bias_table = jnp.einsum("bh,bl->hl", rel_bias, one_hot, precision=lax.Precision.HIGHEST)
    return (one_hot, bias_table)


def spread(bias_table, row_count, col_count):
    full_span = row_count + col_count - 1
    leading = bias_table.shape[:-1]
    tiled_rows = jnp.broadcast_to(bias_table[..., None, :], leading + (row_count, full_span))
    flat_rows = tiled_rows.reshape(leading + (row_count * full_span,))
    flat_rows = jnp.pad(flat_rows, [(0, 0)] * len(leading) + [(0, row_count)])
    skewed = flat_rows.reshape(leading + (row_count, full_span + 1))[..., :col_count]
    return skewed[..., ::-1]


def collapse(matrix, row_count, col_count):
    full_span = row_count + col_count - 1
    leading = matrix.shape[:-2]
    flipped = matrix[..., ::-1]
    padded = jnp.pad(flipped, [(0, 0)] * len(leading) + [(0, 0), (0, row_count)])
    flat_rows = padded.reshape(leading + (row_count * (full_span + 1),))[
        ..., : row_count * full_span
    ]
    return jnp.sum(flat_rows.reshape(leading + (row_count, full_span)), axis=-2)


def shard_group(shard_count, row_count):
    group_size = 1
    while group_size < shard_count and (
        shard_count % group_size != 0 or group_size * row_count < 384
    ):
        group_size += 1
    return group_size


def query_side(
    queries,
    out_grads,
    all_keys,
    all_values,
    key_ids,
    query_ids,
    query_start,
    rel_bias,
    block_rows,
    causal,
):
    row_count, head_count, head_size = queries.shape
    block_count = all_keys.shape[0] // block_rows
    query_pos = query_start + jnp.arange(row_count, dtype=jnp.int32)
    block_ids = jnp.arange(block_count, dtype=jnp.int32)

    def scores_of(block_id):
        key_first = block_id * block_rows
        key_block = lax.dynamic_slice_in_dim(all_keys, key_first, block_rows, 0)
        key_block_ids = lax.dynamic_slice_in_dim(key_ids, key_first, block_rows, 0)
        scores = jnp.einsum("thd,uhd->htu", queries, key_block, preferred_element_type=jnp.float32)
        allowed = query_ids[:, None] == key_block_ids[None, :]
        one_hot = jnp.zeros((1, 1), jnp.float32)
        if causal:
            key_pos = key_first + jnp.arange(block_rows, dtype=jnp.int32)
            allowed = allowed & (query_pos[:, None] >= key_pos[None, :])
            one_hot, bias_table = distance_table(
                rel_bias, query_start - key_first - (block_rows - 1), row_count + block_rows - 1
            )
            scores = scores + spread(bias_table, row_count, block_rows)
        return (jnp.where(allowed[None], scores, -1e30), one_hot)

    def stat_step(running, block_id):
        row_high, total_sum = running
        scores, unused_hot = scores_of(block_id)
        new_high = jnp.maximum(row_high, jnp.max(scores, axis=2))
        total_sum = total_sum * jnp.exp(row_high - new_high) + jnp.sum(
            jnp.exp(scores - new_high[:, :, None]), axis=2
        )
        return ((new_high, total_sum), None)

    start_state = (
        jnp.full((head_count, row_count), -1e30, jnp.float32),
        jnp.zeros((head_count, row_count), jnp.float32),
    )
    (row_high, total_sum), unused_stats = lax.scan(stat_step, start_state, block_ids)

    def weights_of(scores):
        return jnp.exp(scores - row_high[:, :, None]) / total_sum[:, :, None]

    def out_step(summed, block_id):
        scores, unused_hot = scores_of(block_id)
        narrow_weights = weights_of(scores).astype(jnp.bfloat16)
        value_block = lax.dynamic_slice_in_dim(all_values, block_id * block_rows, block_rows, 0)
        return (
            summed
            + jnp.einsum(
                "htu,uhd->thd", narrow_weights, value_block, preferred_element_type=jnp.float32
            ),
            None,
        )

    summed, unused_outs = lax.scan(
        out_step, jnp.zeros((row_count, head_count, head_size), jnp.float32), block_ids
    )
    outputs = summed.astype(jnp.bfloat16)
    row_delta = jnp.einsum("thd,thd->ht", out_grads, outputs, preferred_element_type=jnp.float32)

    def grad_step(running, block_id):
        query_grad, bias_grad_sum = running
        scores, one_hot = scores_of(block_id)
        weights = weights_of(scores)
        narrow_weights = weights.astype(jnp.bfloat16)
        key_block = lax.dynamic_slice_in_dim(all_keys, block_id * block_rows, block_rows, 0)
        value_block = lax.dynamic_slice_in_dim(all_values, block_id * block_rows, block_rows, 0)
        weight_grads = jnp.einsum(
            "thd,uhd->htu", out_grads, value_block, preferred_element_type=jnp.float32
        )
        score_grads = weights * (weight_grads - row_delta[:, :, None])
        narrow_grads = score_grads.astype(jnp.bfloat16)
        query_grad = query_grad + jnp.einsum(
            "htu,uhd->thd", narrow_grads, key_block, preferred_element_type=jnp.float32
        )
        if causal:
            bias_grad_sum = bias_grad_sum + jnp.einsum(
                "hl,bl->bh",
                collapse(score_grads, row_count, block_rows),
                one_hot,
                precision=lax.Precision.HIGHEST,
            )
        key_term = jnp.einsum(
            "htu,thd->uhd", narrow_grads, queries, preferred_element_type=jnp.float32
        )
        value_term = jnp.einsum(
            "htu,thd->uhd", narrow_weights, out_grads, preferred_element_type=jnp.float32
        )
        grad_term = jnp.concatenate(
            [
                key_term.reshape(block_rows, head_count * head_size),
                value_term.reshape(block_rows, head_count * head_size),
            ],
            axis=1,
        ).astype(jnp.bfloat16)
        return ((query_grad, bias_grad_sum), grad_term)

    grad_state = (
        jnp.zeros((row_count, head_count, head_size), jnp.float32),
        jnp.zeros((rel_bias.shape[0], head_count), jnp.float32),
    )
    (query_grad, bias_grad_sum), grad_terms = lax.scan(grad_step, grad_state, block_ids)
    grad_terms = grad_terms.reshape(block_count * block_rows, 2 * head_count * head_size)
    query_grad = query_grad.astype(jnp.bfloat16).reshape(row_count, head_count * head_size)
    return (query_grad, grad_terms, bias_grad_sum, (row_high, total_sum, row_delta))


def on_device(
    q_self,
    k_self,
    v_self,
    out_grad_self,
    q_cross,
    k_cross,
    v_cross,
    out_grad_cross,
    dec_lengths,
    enc_lengths,
    rel_bias,
):
    seq_count = lax.axis_size("seq")
    seq_place = lax.axis_index("seq")
    dec_rows = q_self.shape[1]
    enc_rows = k_cross.shape[1]
    feature_count = q_self.shape[2]
    head_count = feature_count // HEAD_DIM
    dec_total = dec_rows * seq_count
    enc_total = enc_rows * seq_count
    dec_start = seq_place * dec_rows
    dec_ids = example_ids(dec_total, dec_lengths[0])
    enc_ids = example_ids(enc_total, enc_lengths[0])
    my_dec_ids = lax.dynamic_slice_in_dim(dec_ids, dec_start, dec_rows, 0)

    def split_heads(tensor):
        return tensor.reshape(tensor.shape[0] * tensor.shape[1], head_count, HEAD_DIM)

    gathered = (
        lax.all_gather(k_self, "seq", axis=1, tiled=True),
        lax.all_gather(v_self, "seq", axis=1, tiled=True),
        lax.all_gather(k_cross, "seq", axis=1, tiled=True),
        lax.all_gather(v_cross, "seq", axis=1, tiled=True),
    )
    self_group = shard_group(seq_count, dec_rows)
    cross_group = shard_group(seq_count, enc_rows)
    self_dq, self_terms, self_bias, self_stats = query_side(
        split_heads(q_self),
        split_heads(out_grad_self),
        split_heads(gathered[0]),
        split_heads(gathered[1]),
        dec_ids,
        my_dec_ids,
        dec_start,
        rel_bias,
        self_group * dec_rows,
        True,
    )
    cross_dq, cross_terms, unused_bias, cross_stats = query_side(
        split_heads(q_cross),
        split_heads(out_grad_cross),
        split_heads(gathered[2]),
        split_heads(gathered[3]),
        enc_ids,
        my_dec_ids,
        dec_start,
        rel_bias,
        cross_group * enc_rows,
        False,
    )
    self_sums = lax.psum_scatter(
        self_terms.astype(jnp.float32).astype(jnp.bfloat16), "seq", scatter_dimension=0, tiled=True
    ).astype(jnp.float32)
    cross_sums = lax.psum_scatter(
        cross_terms.astype(jnp.float32).astype(jnp.bfloat16), "seq", scatter_dimension=0, tiled=True
    ).astype(jnp.float32)
    self_key_grad = self_sums[:, :feature_count]
    self_value_grad = self_sums[:, feature_count:]
    cross_key_grad = cross_sums[:, :feature_count]
    cross_value_grad = cross_sums[:, feature_count:]
    bias_total = lax.psum(self_bias, ("dp", "seq"))
    bias_grad = bias_total * (1.0 / math.sqrt(lax.axis_size("dp") * dec_total))
    return (
        self_dq.reshape(1, dec_rows, feature_count),
        self_key_grad.reshape(1, dec_rows, feature_count).astype(jnp.bfloat16),
        self_value_grad.reshape(1, dec_rows, feature_count).astype(jnp.bfloat16),
        cross_dq.reshape(1, dec_rows, feature_count),
        cross_key_grad.reshape(1, enc_rows, feature_count).astype(jnp.bfloat16),
        cross_value_grad.reshape(1, enc_rows, feature_count).astype(jnp.bfloat16),
        bias_grad,
    )


def solution(mesh):
    return jax.shard_map(
        on_device,
        mesh=mesh,
        in_specs=(
            P("dp", "seq", "mp"),
            P("dp", "seq", "mp"),
            P("dp", "seq", "mp"),
            P("dp", "seq", "mp"),
            P("dp", "seq", "mp"),
            P("dp", "seq", "mp"),
            P("dp", "seq", "mp"),
            P("dp", "seq", "mp"),
            P("dp", None),
            P("dp", None),
            P(None, "mp"),
        ),
        out_specs=(
            P("dp", "seq", "mp"),
            P("dp", "seq", "mp"),
            P("dp", "seq", "mp"),
            P("dp", "seq", "mp"),
            P("dp", "seq", "mp"),
            P("dp", "seq", "mp"),
            P(None, "mp"),
        ),
        check_vma=False,
    )
```

profile of v0, /device:TPU:2, one launch (start us, length us, event | category | flops | bytes accessed | tf_op | source)
XLA Modules:
  0.0 455.4 jit_solution(5825784003897655049)
XLA Ops:
  17.9 34.6 %all-gather.5.cloned.1.call-done = bf16[1,1024,1024]{2,1,0:T(8,128)(2,1)} async-done(((bf16[1,64,1024]{2,1,0:T(8,128)(2,1)}), bf16[1,1024,1024]{2,1,0:T(8,128)(2,1)}) %all-gather.5.cloned.1.call-update) | async-done | bytes 2097168 | tf_op jit(solution)/shard_map/all_gather | solution.py:215
  52.6 3.9 copy.70
  56.5 31.9 %while.91 = (s32[]{:T(128)}, f32[16,64]{1,0:T(8,128)S(1)}, f32[16,64]{1,0:T(8,128)S(1)}, s32[64]{0:T(128)S(1)}, s32[2]{0:T(128)S(1)}, /*index=5*/s32[1024]{0:T(1...) while((s32[]{:T(128)}, f32[16,64]{1,0:T(8,128)S(1)}, ...), condition=%wide.region_5.6_spmd.clone.clone.clone, body=%wide.region_2.0_spmd.clone.clone.clone.sunk | while | flops 73413688 | bytes 34665884 | solution.py:115
  66.6 2.5 rev.40
  82.6 2.5 rev.40
  88.4 4.1 all-gather.7.cloned.1.call-done
  92.5 3.9 copy.74
  96.4 34.2 %while.92 = (s32[]{:T(128)}, f32[64,16,64]{0,2,1:T(8,128)}, s32[2]{0:T(128)S(1)}, bf16[1024,16,64]{0,2,1:T(8,128)(2,1)}, s32[64]{0:T(128)S(1)}, /*index=5*/s32[1...) while((s32[]{:T(128)}, f32[64,16,64]{0,2,1:T(8,128)}, ...), condition=%wide.region_7.8_spmd.clone.clone.clone, body=%wide.region_6.7_spmd.clone.clone.clone.sunk | while | flops 140648496 | bytes 34098144 | solution.py:132
  109.2 3.4 fusion.213
  126.3 3.4 fusion.213
  131.7 80.7 %while.93 = (s32[]{:T(128)}, f32[64,16,64]{0,2,1:T(8,128)}, f32[32,16]{0,1:T(8,128)S(1)}, bf16[2,512,2048]{2,1,0:T(8,128)(2,1)}, s32[2]{0:T(128)S(1)}, /*index=5...) while((s32[]{:T(128)}, f32[64,16,64]{0,2,1:T(8,128)}, ...), condition=%wide.region_10.11_spmd.clone.clone.clone, body=%wide.region_8.10_spmd.clone.clone.clone.sunk | while | flops 353446976 | bytes 101543680 | solution.py:179
  144.6 2.7 fusion.226
  154.3 2.5 rev.43
  164.8 3.7 reshape.726
  168.9 3.3 constant_dynamic-update-slice_fusion.5
  184.9 2.7 fusion.226
  205.1 3.7 reshape.726
  209.2 3.3 constant_dynamic-update-slice_fusion.5
  212.6 6.7 %copy.79 = bf16[1,2048,1024]{1,2,0:T(8,128)(2,1)} copy(bf16[1,2048,1024]{2,1,0:T(8,128)(2,1)} %all-gather.9.cloned.1.call-done) | data formatting | bytes 8388608 | tf_op jit(solution)/shard_map/all_gather | solution.py:217
  219.4 15.2 %while.88 = (s32[]{:T(128)}, f32[16,64]{1,0:T(8,128)S(1)}, f32[16,64]{1,0:T(8,128)S(1)}, s32[64]{0:T(128)S(1)}, s32[4]{0:T(128)S(1)}, /*index=5*/s32[2048]{0:T(1...) while((s32[]{:T(128)}, f32[16,64]{1,0:T(8,128)S(1)}, ...), condition=%wide.region_17.18_spmd.clone, body=%wide.region_14.17_spmd.clone.sunk | while | flops 69768200 | bytes 5532106 | solution.py:115
  234.6 6.6 %copy.83 = bf16[1,2048,1024]{1,2,0:T(8,128)(2,1)} copy(bf16[1,2048,1024]{2,1,0:T(8,128)(2,1)} %all-gather.11.cloned.1.call-done) | data formatting | bytes 8388608 | tf_op jit(solution)/shard_map/all_gather | solution.py:218
  241.3 16.1 %while.89 = (s32[]{:T(128)}, f32[64,16,64]{0,2,1:T(8,128)S(1)}, s32[4]{0:T(128)S(1)}, bf16[2048,16,64]{0,2,1:T(8,128)(2,1)}, s32[64]{0:T(128)S(1)}, /*index=5*/s...) while((s32[]{:T(128)}, f32[64,16,64]{0,2,1:T(8,128)S(1)}, ...), condition=%wide.region_19.20_spmd.clone, body=%wide.region_18.19_spmd.clone.sunk | while | flops 136478720 | bytes 2834388 | solution.py:132
  242.7 2.6 fusion.191
  246.7 2.6 fusion.191
  250.8 2.5 fusion.191
  254.8 2.6 fusion.191
  257.5 54.1 %while.90 = (s32[]{:T(128)}, f32[64,16,64]{0,2,1:T(8,128)S(1)}, bf16[4,512,2048]{2,1,0:T(8,128)(2,1)}, s32[4]{0:T(128)S(1)}, bf16[2048,16,64]{0,2,1:T(8,128)(2,1...) while((s32[]{:T(128)}, f32[64,16,64]{0,2,1:T(8,128)S(1)}, ...), condition=%wide.region_21.22_spmd.clone, body=%wide.region_20.21_spmd.clone.sunk | while | flops 344621056 | bytes 28396028 | solution.py:179
  266.6 2.9 copy.116
  280.2 2.9 copy.116
  293.6 2.9 copy.116
  307.1 2.9 copy.116
  313.4 130.1 %psum.7 = f32[32,16]{0,1:T(8,128)S(1)} all-reduce(f32[32,16]{0,1:T(8,128)S(1)} %get-tuple-element.693), channel_id=1, replica_groups=mesh['dp'=4,'seq'=16,'mp'=4] {'dp','seq'}, use_global_device_ids=true, to_apply=%region_23.24 | all-reduce | flops 512 | bytes 4096 | tf_op jit(solution)/shard_map/psum | solution.py:256
  (310 shorter events, 181.8 us)
Async XLA Ops:
  7.2 9.6 %copy-start.19 = (bf16[1,64,1024]{2,1,0:T(8,128)(2,1)S(1)}, bf16[1,64,1024]{2,1,0:T(8,128)(2,1)}, u32[]{:S(2)}) copy-start(bf16[1,64,1024]{2,1,0:T(8,128)(2,1)} %param.27) | copy-start | bytes 393220
  7.2 45.4 %all-gather.5.cloned.1.call-start = ((), (), s32[]{:S(2)}) async-start(), calls=%async_computation.2 | async-start | bytes 2228224 | tf_op jit(solution)/shard_map/all_gather | solution.py:215
  7.9 84.5 %all-gather.7.cloned.1.call-start = ((), (), s32[]{:S(2)}) async-start(), calls=%async_computation.3 | async-start | bytes 2228224 | tf_op jit(solution)/shard_map/all_gather | solution.py:216
  8.7 203.9 %all-gather.9.cloned.1.call-start = ((), (), s32[]{:S(2)}) async-start(), calls=%async_computation.5 | async-start | bytes 4456448 | tf_op jit(solution)/shard_map/all_gather | solution.py:217
  9.4 225.2 %all-gather.11.cloned.1.call-start = ((), (), s32[]{:S(2)}) async-start(), calls=%async_computation.6 | async-start | bytes 4456448 | tf_op jit(solution)/shard_map/all_gather | solution.py:218
  10.0 435.0 %reduce-scatter.3.cloned.1.call-start = ((), (), s32[]{:S(2)}) async-start(), calls=%async_computation.4 | async-start | bytes 4456448 | tf_op jit(solution)/shard_map/reduce_scatter | solution.py:246
  17.0 39.5 %copy-start.7 = (bf16[1,64,1024]{1,2,0:T(8,128)(2,1)}, bf16[1,64,1024]{1,2,0:T(8,128)(2,1)S(1)}, u32[]{:S(2)}) copy-start(bf16[1,64,1024]{1,2,0:T(8,128)(2,1)S(1)} %copy.81) | copy-start | bytes 393220
  17.9 38.6 %copy-start.12 = (f32[32,16]{0,1:T(8,128)S(1)}, f32[32,16]{0,1:T(8,128)}, u32[]{:S(2)}) copy-start(f32[32,16]{0,1:T(8,128)} %param.33) | copy-start | bytes 6148
  81.0 1.6 slice-start
  105.1 1.6 slice-start.1
  106.7 2.5 copy-start.15
  122.2 1.6 slice-start.1
  123.8 2.5 copy-start.15
  131.9 12.7 %copy-start.9 = (bf16[64,16,64]{0,2,1:T(8,128)(2,1)}, bf16[64,16,64]{0,2,1:T(8,128)(2,1)S(1)}, u32[]{:S(2)}) copy-start(bf16[64,16,64]{0,2,1:T(8,128)(2,1)S(1)} %get-tuple-element.1967) | copy-start | bytes 393220 | tf_op jit(solution)/shard_map/while
  140.5 1.6 slice-start.2
  147.3 1.6 copy-start.2
  148.8 1.6 copy-start
  148.9 1.7 copy-start.3
  168.9 3.3 copy-start.10
  172.3 12.7 %copy-start.9 = (bf16[64,16,64]{0,2,1:T(8,128)(2,1)}, bf16[64,16,64]{0,2,1:T(8,128)(2,1)S(1)}, u32[]{:S(2)}) copy-start(bf16[64,16,64]{0,2,1:T(8,128)(2,1)S(1)} %get-tuple-element.1967) | copy-start | bytes 393220 | tf_op jit(solution)/shard_map/while
  187.6 1.6 copy-start.2
  189.2 1.7 copy-start.3
  209.2 3.3 copy-start.10
  212.5 6.9 %copy-start.11 = (bf16[64,16,64]{2,0,1:T(8,128)(2,1)S(1)}, bf16[64,16,64]{2,0,1:T(8,128)(2,1)}, u32[]{:S(2)}) copy-start(bf16[64,16,64]{2,0,1:T(8,128)(2,1)} %copy.82) | copy-start | bytes 393220
  212.5 6.8 %copy-start.13 = (f32[16,64]{1,0:T(8,128)S(1)}, f32[16,64]{1,0:T(8,128)}, u32[]{:S(2)}) copy-start(f32[16,64]{1,0:T(8,128)} %custom-call.5) | copy-start | bytes 12292
  212.5 6.8 %copy-start.17 = (f32[16,64]{1,0:T(8,128)S(1)}, f32[16,64]{1,0:T(8,128)}, u32[]{:S(2)}) copy-start(f32[16,64]{1,0:T(8,128)} %custom-call.6) | copy-start | bytes 12292
  212.5 6.8 %copy-start.18 = (s32[2048]{0:T(1024)S(1)}, s32[2048]{0:T(1024)}, u32[]{:S(2)}) copy-start(s32[2048]{0:T(1024)} %convert_reduce_fusion) | copy-start | bytes 24580
  212.5 234.2 %reduce-scatter.5.cloned.1.call-start = ((), (), s32[]{:S(2)}) async-start(), calls=%async_computation.7 | async-start | bytes 8912896 | tf_op jit(solution)/shard_map/reduce_scatter | solution.py:249
  234.6 6.7 %copy-start.14 = (f32[64,16,64]{0,2,1:T(8,128)S(1)}, f32[64,16,64]{0,2,1:T(8,128)}, u32[]{:S(2)}) copy-start(f32[64,16,64]{0,2,1:T(8,128)} %custom-call.7) | copy-start | bytes 786436
  241.3 16.1 %copy-start.1 = (bf16[1,64,1024]{1,2,0:T(8,128)(2,1)S(1)}, bf16[1,64,1024]{1,2,0:T(8,128)(2,1)}, u32[]{:S(2)}) copy-start(bf16[1,64,1024]{1,2,0:T(8,128)(2,1)} %copy.84) | copy-start | bytes 393220
  241.3 16.2 %copy-start.6 = (f32[64,16,64]{0,2,1:T(8,128)S(1)}, f32[64,16,64]{0,2,1:T(8,128)}, u32[]{:S(2)}) copy-start(f32[64,16,64]{0,2,1:T(8,128)} %custom-call.8) | copy-start | bytes 786436
  241.3 16.2 %copy-start.8 = (bf16[1,64,1024]{1,2,0:T(8,128)(2,1)S(1)}, bf16[1,64,1024]{1,2,0:T(8,128)(2,1)}, u32[]{:S(2)}) copy-start(bf16[1,64,1024]{1,2,0:T(8,128)(2,1)} %copy-done.7) | copy-start | bytes 393220
  (8 other events, 9.2 us)
Sparse Core Ops, SparseCore 0:
  9.8 42.6 all-gather.4
  54.4 38.0 all-gather.6
  94.3 40.5 all-gather.8
  136.5 40.8 all-gather.10
  212.6 61.6 reduce-scatter.2
  311.7 69.7 reduce-scatter.4
where the time goes:
time: 458 us; the launch traced here: 455 us
  local copies, waits for them, and re-layouts  170 us (37%)
  blocking collectives  130 us (28%)
  matrix products  67.9 us (15%)
  waiting for transfers between devices  41.4 us (9%)
  other arithmetic  17.8 us (4%)
  between operations  14.5 us (3%)
  loops' own time  13.3 us (3%)
    psum x1, blocking collectives, on_device(): bias_total = lax.psum(self_bias, ('dp', 'seq'))  130 us
    all_gather x1, waiting for transfers between devices, on_device(): lax.all_gather(k_self, 'seq', axis=1, tiled=True)  34.6 us
    dynamic_update_slice x12, local copies, waits for them, and re-layouts, query_side(): lax.scan(grad_step, grad_state, block_ids)  29.1 us
    dot_general x12, matrix products, scores_of(): jnp.einsum('thd,uhd->htu', queries, key_block, preferred_element_type=jnp...  24.8 us
    dot_general x6, matrix products, out_step(): jnp.einsum('htu,uhd->thd', narrow_weights, value_block, preferred_element...  17.1 us
    rev x6, local copies, waits for them, and re-layouts, spread(): return skewed[..., ::-1]  15.1 us
    reshape x6, local copies, waits for them, and re-layouts, spread(): flat_rows = tiled_rows.reshape(leading + (row_count * full_span,))  14.9 us
    reshape x6, local copies, waits for them, and re-layouts, spread(): flat_rows.reshape(leading + (row_count, full_span + 1))[..., :col_count]  14.6 us
  transfers between devices with their start and end apart: 6, of which 2 were waited for; matrix products, arithmetic and copies ran while one was open for 52% of the time, Pallas kernels for 0%

commit v1 on v0

--- a/solution.py
+++ b/solution.py
@@ -253,7 +253,7 @@
     self_value_grad = self_sums[:, feature_count:]
     cross_key_grad = cross_sums[:, :feature_count]
     cross_value_grad = cross_sums[:, feature_count:]
-    bias_total = lax.psum(self_bias, ("dp", "seq"))
+    bias_total = lax.psum(lax.psum(self_bias, "seq"), "dp")
     bias_grad = bias_total * (1.0 / math.sqrt(lax.axis_size("dp") * dec_total))
     return (
         self_dq.reshape(1, dec_rows, feature_count),

time: 458 us -> 393 us (0.86)
  blocking collectives: 130 us -> 36.4 us
  waiting for transfers between devices: 41.4 us -> 69.6 us
    psum x1 -> x2, blocking collectives: 130 us -> 36.4 us  [on_device(): bias_total = lax.psum(lax.psum(self_bias, 'seq'), 'dp')]
    reduce_scatter x1, waiting for transfers between devices: 0.01 us -> 28 us  [on_device(): lax.psum_scatter(cross_terms.astype(jnp.float32).astype(jnp.bfloat16), 's...]
  transfers between devices with their start and end apart: 6 -> 6, of which waited for: 2 -> 3; matrix products, arithmetic and copies ran while one was open for 52% -> 60% of each run, Pallas kernels for 0% -> 0%
where the time goes in v1:
time: 393 us; the launch traced here: 390 us
  local copies, waits for them, and re-layouts  170 us (43%)
  waiting for transfers between devices  69.6 us (18%)
  matrix products  67.9 us (17%)
  blocking collectives  36.4 us (9%)
  other arithmetic  17.9 us (5%)
  between operations  14.5 us (4%)
  loops' own time  13 us (3%)
    psum x2, blocking collectives, on_device(): bias_total = lax.psum(lax.psum(self_bias, 'seq'), 'dp')  36.4 us
    all_gather x1, waiting for transfers between devices, on_device(): lax.all_gather(k_self, 'seq', axis=1, tiled=True)  34.6 us
    dynamic_update_slice x12, local copies, waits for them, and re-layouts, query_side(): lax.scan(grad_step, grad_state, block_ids)  29.1 us
    reduce_scatter x1, waiting for transfers between devices, on_device(): lax.psum_scatter(cross_terms.astype(jnp.float32).astype(jnp.bfloat16), 's...  28 us
    dot_general x12, matrix products, scores_of(): jnp.einsum('thd,uhd->htu', queries, key_block, preferred_element_type=jnp...  24.8 us
    dot_general x6, matrix products, out_step(): jnp.einsum('htu,uhd->thd', narrow_weights, value_block, preferred_element...  17.1 us
    rev x6, local copies, waits for them, and re-layouts, spread(): return skewed[..., ::-1]  15 us
    reshape x6, local copies, waits for them, and re-layouts, spread(): flat_rows = tiled_rows.reshape(leading + (row_count * full_span,))  14.9 us
  transfers between devices with their start and end apart: 6, of which 3 were waited for; matrix products, arithmetic and copies ran while one was open for 60% of the time, Pallas kernels for 0%

profile of v1, /device:TPU:2, one launch (start us, length us, event | category | flops | bytes accessed | tf_op | source)
XLA Modules:
  0.0 389.7 jit_solution(881093316746928909)
XLA Ops:
  17.9 34.6 %all-gather.5.cloned.1.call-done = bf16[1,1024,1024]{2,1,0:T(8,128)(2,1)} async-done(((bf16[1,64,1024]{2,1,0:T(8,128)(2,1)}), bf16[1,1024,1024]{2,1,0:T(8,128)(2,1)}) %all-gather.5.cloned.1.call-update) | async-done | bytes 2097168 | tf_op jit(solution)/shard_map/all_gather | solution.py:215
  52.6 3.9 %copy.70 = bf16[1,1024,1024]{1,2,0:T(8,128)(2,1)} copy(bf16[1,1024,1024]{2,1,0:T(8,128)(2,1)} %all-gather.5.cloned.1.call-done) | data formatting | bytes 4194304 | tf_op jit(solution)/shard_map/all_gather | solution.py:215
  56.5 31.7 %while.91 = (s32[]{:T(128)}, f32[16,64]{1,0:T(8,128)S(1)}, f32[16,64]{1,0:T(8,128)S(1)}, s32[64]{0:T(128)S(1)}, s32[2]{0:T(128)S(1)}, /*index=5*/s32[1024]{0:T(1...) while((s32[]{:T(128)}, f32[16,64]{1,0:T(8,128)S(1)}, ...), condition=%wide.region_5.6_spmd.clone.clone.clone, body=%wide.region_2.0_spmd.clone.clone.clone.sunk | while | flops 73413688 | bytes 34665884 | solution.py:115
  88.2 4.3 %all-gather.7.cloned.1.call-done = bf16[1,1024,1024]{2,1,0:T(8,128)(2,1)} async-done(((bf16[1,64,1024]{2,1,0:T(8,128)(2,1)}), bf16[1,1024,1024]{2,1,0:T(8,128)(2,1)}) %all-gather.7.cloned.1.call-update) | async-done | bytes 2097168 | tf_op jit(solution)/shard_map/all_gather | solution.py:216
  92.5 3.9 %copy.74 = bf16[1,1024,1024]{1,2,0:T(8,128)(2,1)} copy(bf16[1,1024,1024]{2,1,0:T(8,128)(2,1)} %all-gather.7.cloned.1.call-done) | data formatting | bytes 4194304 | tf_op jit(solution)/shard_map/all_gather | solution.py:216
  96.4 33.9 %while.92 = (s32[]{:T(128)}, f32[64,16,64]{0,2,1:T(8,128)}, s32[2]{0:T(128)S(1)}, bf16[1024,16,64]{0,2,1:T(8,128)(2,1)}, s32[64]{0:T(128)S(1)}, /*index=5*/s32[1...) while((s32[]{:T(128)}, f32[64,16,64]{0,2,1:T(8,128)}, ...), condition=%wide.region_7.8_spmd.clone.clone.clone, body=%wide.region_6.7_spmd.clone.clone.clone.sunk | while | flops 140648496 | bytes 34098144 | solution.py:132
  109.1 3.4 fusion.213
  126.1 3.4 fusion.213
  131.5 81.0 %while.93 = (s32[]{:T(128)}, f32[64,16,64]{0,2,1:T(8,128)}, f32[32,16]{0,1:T(8,128)S(1)}, bf16[2,512,2048]{2,1,0:T(8,128)(2,1)}, s32[2]{0:T(128)S(1)}, /*index=5...) while((s32[]{:T(128)}, f32[64,16,64]{0,2,1:T(8,128)}, ...), condition=%wide.region_10.11_spmd.clone.clone.clone, body=%wide.region_8.10_spmd.clone.clone.clone.sunk | while | flops 353446976 | bytes 101543680 | solution.py:179
  144.4 2.7 fusion.226
  164.7 3.8 reshape.726
  168.9 3.3 constant_dynamic-update-slice_fusion.5
  184.9 2.7 fusion.226
  194.5 2.5 rev.43
  205.1 3.7 reshape.726
  209.2 3.3 constant_dynamic-update-slice_fusion.5
  212.6 6.7 %copy.79 = bf16[1,2048,1024]{1,2,0:T(8,128)(2,1)} copy(bf16[1,2048,1024]{2,1,0:T(8,128)(2,1)} %all-gather.9.cloned.1.call-done) | data formatting | bytes 8388608 | tf_op jit(solution)/shard_map/all_gather | solution.py:217
  219.4 15.2 %while.88 = (s32[]{:T(128)}, f32[16,64]{1,0:T(8,128)S(1)}, f32[16,64]{1,0:T(8,128)S(1)}, s32[64]{0:T(128)S(1)}, s32[4]{0:T(128)S(1)}, /*index=5*/s32[2048]{0:T(1...) while((s32[]{:T(128)}, f32[16,64]{1,0:T(8,128)S(1)}, ...), condition=%wide.region_17.18_spmd.clone, body=%wide.region_14.17_spmd.clone.sunk | while | flops 69768200 | bytes 5532106 | solution.py:115
  234.7 6.6 %copy.83 = bf16[1,2048,1024]{1,2,0:T(8,128)(2,1)} copy(bf16[1,2048,1024]{2,1,0:T(8,128)(2,1)} %all-gather.11.cloned.1.call-done) | data formatting | bytes 8388608 | tf_op jit(solution)/shard_map/all_gather | solution.py:218
  241.3 16.1 %while.89 = (s32[]{:T(128)}, f32[64,16,64]{0,2,1:T(8,128)S(1)}, s32[4]{0:T(128)S(1)}, bf16[2048,16,64]{0,2,1:T(8,128)(2,1)}, s32[64]{0:T(128)S(1)}, /*index=5*/s...) while((s32[]{:T(128)}, f32[64,16,64]{0,2,1:T(8,128)S(1)}, ...), condition=%wide.region_19.20_spmd.clone, body=%wide.region_18.19_spmd.clone.sunk | while | flops 136478720 | bytes 2834388 | solution.py:132
  242.7 2.6 fusion.191
  246.7 2.6 fusion.191
  250.8 2.5 fusion.191
  254.8 2.6 fusion.191
  257.5 54.1 %while.90 = (s32[]{:T(128)}, f32[64,16,64]{0,2,1:T(8,128)S(1)}, bf16[4,512,2048]{2,1,0:T(8,128)(2,1)}, s32[4]{0:T(128)S(1)}, bf16[2048,16,64]{0,2,1:T(8,128)(2,1...) while((s32[]{:T(128)}, f32[64,16,64]{0,2,1:T(8,128)S(1)}, ...), condition=%wide.region_21.22_spmd.clone, body=%wide.region_20.21_spmd.clone.sunk | while | flops 344621056 | bytes 28396028 | solution.py:179
  266.7 3.0 copy.116
  280.2 2.9 copy.116
  293.7 2.9 copy.116
  307.2 2.9 copy.116
  313.5 25.8 %psum.14 = f32[32,16]{0,1:T(8,128)S(1)} all-reduce(f32[32,16]{0,1:T(8,128)S(1)} %get-tuple-element.693), channel_id=1, replica_groups=mesh['dp'=4,'seq'=16,'mp'=4] {'seq'}, use_global_device_ids=true, to_apply=%region_23.24 | all-reduce | flops 512 | bytes 4096 | tf_op jit(solution)/shard_map/psum | solution.py:256
  339.3 10.6 %psum.15 = f32[32,16]{0,1:T(8,128)S(1)} all-reduce(f32[32,16]{0,1:T(8,128)S(1)} %psum.14), channel_id=1, replica_groups=mesh['dp'=4,'seq'=16,'mp'=4] {'dp'}, use_global_device_ids=true, to_apply=%region_24.25 | all-reduce | flops 512 | bytes 4096 | tf_op jit(solution)/shard_map/psum | solution.py:256
  353.0 28.0 %reduce-scatter.5.cloned.1.call-done = bf16[128,2048]{1,0:T(8,128)(2,1)} async-done(((bf16[2048,2048]{1,0:T(8,128)(2,1)}), bf16[128,2048]{1,0:T(8,128)(2,1)}) %reduce-scatter.5.cloned.1.call-update) | async-done | bytes 524304 | tf_op jit(solution)/shard_map/reduce_scatter | solution.py:249
  (311 shorter events, 186.9 us)
Async XLA Ops:
  7.2 9.6 %copy-start.19 = (bf16[1,64,1024]{2,1,0:T(8,128)(2,1)S(1)}, bf16[1,64,1024]{2,1,0:T(8,128)(2,1)}, u32[]{:S(2)}) copy-start(bf16[1,64,1024]{2,1,0:T(8,128)(2,1)} %param.27) | copy-start | bytes 393220
  7.2 45.4 %all-gather.5.cloned.1.call-start = ((), (), s32[]{:S(2)}) async-start(), calls=%async_computation.2 | async-start | bytes 2228224 | tf_op jit(solution)/shard_map/all_gather | solution.py:215
  7.9 84.5 %all-gather.7.cloned.1.call-start = ((), (), s32[]{:S(2)}) async-start(), calls=%async_computation.3 | async-start | bytes 2228224 | tf_op jit(solution)/shard_map/all_gather | solution.py:216
  8.7 203.9 %all-gather.9.cloned.1.call-start = ((), (), s32[]{:S(2)}) async-start(), calls=%async_computation.5 | async-start | bytes 4456448 | tf_op jit(solution)/shard_map/all_gather | solution.py:217
  9.4 225.3 %all-gather.11.cloned.1.call-start = ((), (), s32[]{:S(2)}) async-start(), calls=%async_computation.6 | async-start | bytes 4456448 | tf_op jit(solution)/shard_map/all_gather | solution.py:218
  10.0 341.4 %reduce-scatter.3.cloned.1.call-start = ((), (), s32[]{:S(2)}) async-start(), calls=%async_computation.4 | async-start | bytes 4456448 | tf_op jit(solution)/shard_map/reduce_scatter | solution.py:246
  17.0 39.5 %copy-start.7 = (bf16[1,64,1024]{1,2,0:T(8,128)(2,1)}, bf16[1,64,1024]{1,2,0:T(8,128)(2,1)S(1)}, u32[]{:S(2)}) copy-start(bf16[1,64,1024]{1,2,0:T(8,128)(2,1)S(1)} %copy.81) | copy-start | bytes 393220
  17.9 38.6 %copy-start.12 = (f32[32,16]{0,1:T(8,128)S(1)}, f32[32,16]{0,1:T(8,128)}, u32[]{:S(2)}) copy-start(f32[32,16]{0,1:T(8,128)} %param.33) | copy-start | bytes 6148
  64.9 1.6 slice-start
  106.6 2.5 copy-start.15
  122.0 1.6 slice-start.1
  123.6 2.5 copy-start.15
  131.7 12.7 %copy-start.9 = (bf16[64,16,64]{0,2,1:T(8,128)(2,1)}, bf16[64,16,64]{0,2,1:T(8,128)(2,1)S(1)}, u32[]{:S(2)}) copy-start(bf16[64,16,64]{0,2,1:T(8,128)(2,1)S(1)} %get-tuple-element.1967) | copy-start | bytes 393220 | tf_op jit(solution)/shard_map/while
  140.3 1.6 slice-start.2
  147.0 1.6 copy-start.2
  148.6 1.7 copy-start.3
  168.9 3.3 copy-start.10
  172.2 12.7 %copy-start.9 = (bf16[64,16,64]{0,2,1:T(8,128)(2,1)}, bf16[64,16,64]{0,2,1:T(8,128)(2,1)S(1)}, u32[]{:S(2)}) copy-start(bf16[64,16,64]{0,2,1:T(8,128)(2,1)S(1)} %get-tuple-element.1967) | copy-start | bytes 393220 | tf_op jit(solution)/shard_map/while
  180.8 1.6 slice-start.2
  187.5 1.6 copy-start.2
  189.1 1.6 copy-start
  189.1 1.7 copy-start.3
  209.2 3.3 copy-start.10
  212.5 6.9 %copy-start.11 = (bf16[64,16,64]{2,0,1:T(8,128)(2,1)S(1)}, bf16[64,16,64]{2,0,1:T(8,128)(2,1)}, u32[]{:S(2)}) copy-start(bf16[64,16,64]{2,0,1:T(8,128)(2,1)} %copy.82) | copy-start | bytes 393220
  212.5 6.9 %copy-start.13 = (f32[16,64]{1,0:T(8,128)S(1)}, f32[16,64]{1,0:T(8,128)}, u32[]{:S(2)}) copy-start(f32[16,64]{1,0:T(8,128)} %custom-call.5) | copy-start | bytes 12292
  212.5 6.9 %copy-start.17 = (f32[16,64]{1,0:T(8,128)S(1)}, f32[16,64]{1,0:T(8,128)}, u32[]{:S(2)}) copy-start(f32[16,64]{1,0:T(8,128)} %custom-call.6) | copy-start | bytes 12292
  212.5 6.9 %copy-start.18 = (s32[2048]{0:T(1024)S(1)}, s32[2048]{0:T(1024)}, u32[]{:S(2)}) copy-start(s32[2048]{0:T(1024)} %convert_reduce_fusion) | copy-start | bytes 24580
  212.5 168.5 %reduce-scatter.5.cloned.1.call-start = ((), (), s32[]{:S(2)}) async-start(), calls=%async_computation.7 | async-start | bytes 8912896 | tf_op jit(solution)/shard_map/reduce_scatter | solution.py:249
  234.6 6.6 %copy-start.14 = (f32[64,16,64]{0,2,1:T(8,128)S(1)}, f32[64,16,64]{0,2,1:T(8,128)}, u32[]{:S(2)}) copy-start(f32[64,16,64]{0,2,1:T(8,128)} %custom-call.7) | copy-start | bytes 786436
  241.3 16.1 %copy-start.1 = (bf16[1,64,1024]{1,2,0:T(8,128)(2,1)S(1)}, bf16[1,64,1024]{1,2,0:T(8,128)(2,1)}, u32[]{:S(2)}) copy-start(bf16[1,64,1024]{1,2,0:T(8,128)(2,1)} %copy.84) | copy-start | bytes 393220
  241.3 16.2 %copy-start.6 = (f32[64,16,64]{0,2,1:T(8,128)S(1)}, f32[64,16,64]{0,2,1:T(8,128)}, u32[]{:S(2)}) copy-start(f32[64,16,64]{0,2,1:T(8,128)} %custom-call.8) | copy-start | bytes 786436
  241.3 16.2 %copy-start.8 = (bf16[1,64,1024]{1,2,0:T(8,128)(2,1)S(1)}, bf16[1,64,1024]{1,2,0:T(8,128)(2,1)}, u32[]{:S(2)}) copy-start(bf16[1,64,1024]{1,2,0:T(8,128)(2,1)} %copy-done.7) | copy-start | bytes 393220
  (8 other events, 9.2 us)
Sparse Core Ops, SparseCore 0:
  9.8 42.6 all-gather.4
  54.4 38.0 all-gather.6
  94.3 40.5 all-gather.8
  136.6 40.8 all-gather.10
  212.6 61.5 reduce-scatter.2
  311.7 69.2 reduce-scatter.4
